TPU v7x, 256 devices: a whole 4x4x8 slice. The times are simulated.
256 devices in a mesh: context: 32 (over x, z), mp: 8 (over y, core).
Axes of the slice: x: 4, y: 4, z: 8, core: 2. Of those that a mesh axis runs over, the one named last changes fastest.
Arguments:
- queries: bfloat16 [32768, 2048], P('context', 'mp'), may hold values from -32 to 32
- keys: bfloat16 [32768, 1024], P('context', 'mp'), may hold values from -32 to 32
- values: bfloat16 [32768, 1024], P('context', 'mp'), may hold values from -6 to 6
- out_grad: bfloat16 [32768, 5376], P(('context', 'mp')), may hold values from -24 to 24
- out_weight: bfloat16 [5376, 2048], P(None, 'mp'), may hold values from -0.125 to 0.125
Outputs:
- query_grad: bfloat16 [32768, 2048], P('context', 'mp')
- key_grad: bfloat16 [32768, 1024], P('context', 'mp')
- value_grad: bfloat16 [32768, 1024], P('context', 'mp')
- weight_grad: bfloat16 [5376, 2048], P('context', 'mp')
All inputs are finite; a program needn't handle non-finite values.
Results may differ from a plain program's by a relative error of at most 0.02.
Values may be sent and summed in bfloat16 or wider, within the bound.
A program may use at most 128 MiB of HBM per device.

v0:
```python
import jax
import jax.numpy as jnp
from jax import lax
from jax.sharding import PartitionSpec as P

HEAD_SIZE = 128
WINDOW_KEYS = 512
SCALE = 168.0 ** (-0.5)
NEG = -1e30


def shifted(x, axis, by):
    devices = lax.axis_size(axis)
    pairs = [(i, i + by) for i in range(devices) if 0 <= i + by < devices]
    return lax.ppermute(x, axis, pairs)


def band_grads(query_rows_block, key_rows_block, value_rows_block, output_grad_rows, key_start):
    rows = query_rows_block.shape[0]
    span = key_rows_block.shape[0]
    scores = (
        jnp.einsum(
            "qhgd,khd->hgqk", query_rows_block, key_rows_block, preferred_element_type=jnp.float32
        )
        * SCALE
    )
    qpos = jnp.arange(rows, dtype=jnp.int32)[:, None]
    kpos = jnp.arange(span, dtype=jnp.int32)[None, :]
    allowed = (kpos > qpos) & (kpos <= qpos + (span - rows)) & (kpos + key_start >= 0)
    scores = jnp.where(allowed, scores, NEG)
    top = jnp.max(scores, axis=-1, keepdims=True)
    weights = jnp.exp(scores - top)
    prob = weights / jnp.sum(weights, axis=-1, keepdims=True)
    prob_b = prob.astype(jnp.bfloat16)
    attn = jnp.einsum(
        "hgqk,khd->qhgd", prob_b, value_rows_block, preferred_element_type=jnp.float32
    ).astype(jnp.bfloat16)
    delta = jnp.sum(output_grad_rows.astype(jnp.float32) * attn.astype(jnp.float32), axis=-1)
    delta = jnp.transpose(delta, (1, 2, 0))[..., None]
    dprob = jnp.einsum(
        "qhgd,khd->hgqk", output_grad_rows, value_rows_block, preferred_element_type=jnp.float32
    )
    dscore = (prob * (dprob - delta) * SCALE).astype(jnp.bfloat16)
    dq = jnp.einsum("hgqk,khd->qhgd", dscore, key_rows_block, preferred_element_type=jnp.float32)
    key_gradient = jnp.einsum(
        "hgqk,qhgd->khd", dscore, query_rows_block, preferred_element_type=jnp.float32
    )
    value_gradient = jnp.einsum(
        "hgqk,qhgd->khd", prob_b, output_grad_rows, preferred_element_type=jnp.float32
    )
    return (dq, attn, key_gradient, value_gradient)


def shards(queries, keys, values, out_grad, out_weight):
    shard = queries.shape[0]
    kv_local = keys.shape[1] // HEAD_SIZE
    q_local = queries.shape[1] // HEAD_SIZE
    query_group = q_local // kv_local
    block_index = WINDOW_KEYS // 2
    root = lax.axis_index("context") * shard - WINDOW_KEYS
    prev_keys, prev_values = shifted((keys, values), "context", 1)
    prev_keys = prev_keys[shard - WINDOW_KEYS :]
    prev_values = prev_values[shard - WINDOW_KEYS :]
    key_buf = jnp.concatenate([prev_keys, keys], 0)
    value_buf = jnp.concatenate([prev_values, values], 0)
    grad_full = lax.all_gather(out_grad, "mp", axis=0, tiled=True)
    output_gradient = jnp.dot(grad_full, out_weight, preferred_element_type=jnp.float32).astype(
        jnp.bfloat16
    )

    def step(index, carry):
        dq_all, attn_all, key_gradient_total, value_gradient_total = carry
        start_position = index * block_index
        query_rows_block = lax.dynamic_slice_in_dim(
            queries, start_position, block_index, 0
        ).reshape(block_index, kv_local, query_group, HEAD_SIZE)
        output_grad_rows = lax.dynamic_slice_in_dim(
            output_gradient, start_position, block_index, 0
        ).reshape(block_index, kv_local, query_group, HEAD_SIZE)
        key_rows_block = lax.dynamic_slice_in_dim(
            key_buf, start_position, WINDOW_KEYS + block_index, 0
        ).reshape(WINDOW_KEYS + block_index, kv_local, HEAD_SIZE)
        value_rows_block = lax.dynamic_slice_in_dim(
            value_buf, start_position, WINDOW_KEYS + block_index, 0
        ).reshape(WINDOW_KEYS + block_index, kv_local, HEAD_SIZE)
        dq, attn, key_gradient, value_gradient = band_grads(
            query_rows_block,
            key_rows_block,
            value_rows_block,
            output_grad_rows,
            root + start_position,
        )
        dq_all = lax.dynamic_update_slice_in_dim(
            dq_all, dq.reshape(block_index, q_local * HEAD_SIZE), start_position, 0
        )
        attn_all = lax.dynamic_update_slice_in_dim(
            attn_all, attn.reshape(block_index, q_local * HEAD_SIZE), start_position, 0
        )
        earlier_keys = lax.dynamic_slice_in_dim(
            key_gradient_total, start_position, WINDOW_KEYS + block_index, 0
        )
        earlier_values = lax.dynamic_slice_in_dim(
            value_gradient_total, start_position, WINDOW_KEYS + block_index, 0
        )
        key_gradient_total = lax.dynamic_update_slice_in_dim(
            key_gradient_total,
            earlier_keys + key_gradient.reshape(WINDOW_KEYS + block_index, kv_local * HEAD_SIZE),
            start_position,
            0,
        )
        value_gradient_total = lax.dynamic_update_slice_in_dim(
            value_gradient_total,
            earlier_values
            + value_gradient.reshape(WINDOW_KEYS + block_index, kv_local * HEAD_SIZE),
            start_position,
            0,
        )
        return (dq_all, attn_all, key_gradient_total, value_gradient_total)

    start_state = (
        jnp.zeros((shard, q_local * HEAD_SIZE), jnp.float32),
        jnp.zeros((shard, q_local * HEAD_SIZE), jnp.bfloat16),
        jnp.zeros((WINDOW_KEYS + shard, kv_local * HEAD_SIZE), jnp.float32),
        jnp.zeros((WINDOW_KEYS + shard, kv_local * HEAD_SIZE), jnp.float32),
    )
    dq_all, attn_all, key_gradient_total, value_gradient_total = lax.fori_loop(
        0, shard // block_index, step, start_state
    )
    back_keys, back_values = (
        shifted(key_gradient_total[:WINDOW_KEYS].astype(jnp.bfloat16), "context", -1).astype(
            jnp.float32
        ),
        shifted(value_gradient_total[:WINDOW_KEYS].astype(jnp.bfloat16), "context", -1).astype(
            jnp.float32
        ),
    )
    own_keys = key_gradient_total[WINDOW_KEYS:]
    own_values = value_gradient_total[WINDOW_KEYS:]
    key_grad = jnp.concatenate(
        [own_keys[: shard - WINDOW_KEYS], own_keys[shard - WINDOW_KEYS :] + back_keys], 0
    ).astype(jnp.bfloat16)
    value_grad = jnp.concatenate(
        [own_values[: shard - WINDOW_KEYS], own_values[shard - WINDOW_KEYS :] + back_values], 0
    ).astype(jnp.bfloat16)
    query_grad = dq_all.astype(jnp.bfloat16)
    weight_grad = lax.psum_scatter(
        lax.dot_general(
            grad_full, attn_all, (((0,), (0,)), ((), ())), preferred_element_type=jnp.float32
        ),
        "context",
        scatter_dimension=0,
        tiled=True,
    ).astype(jnp.bfloat16)
    return (query_grad, key_grad, value_grad, weight_grad)


def solution(mesh):
    return jax.shard_map(
        shards,
        mesh=mesh,
        in_specs=(
            P("context", "mp"),
            P("context", "mp"),
            P("context", "mp"),
            P(("context", "mp"), None),
            P(None, "mp"),
        ),
        out_specs=(P("context", "mp"), P("context", "mp"), P("context", "mp"), P("context", "mp")),
        check_vma=False,
    )
```

profile of v0, /device:TPU:8, one launch (start us, length us, event | category | flops | bytes accessed | tf_op | source)
XLA Modules:
  0.0 475.2 jit_solution(9497821260364624964)
XLA Ops:
  8.0 4.7 collective-permute-start
  12.7 3.1 collective-permute-start.1
  15.8 3.2 collective-permute-done
  19.9 3.6 collective-permute-done.1
  25.0 50.4 %all-gather.2.cloned.1.call-done = bf16[1024,5376]{1,0:T(8,128)(2,1)} async-done(((bf16[128,5376]{1,0:T(8,128)(2,1)}), bf16[1024,5376]{1,0:T(8,128)(2,1)}) %all-gather.2.cloned.1.call-update) | async-done | bytes 11010064 | tf_op jit(solution)/shard_map/all_gather | solution.py:66
  75.4 7.9 %convolution_convert_fusion.1 = bf16[1024,256]{1,0:T(8,128)(2,1)} fusion(bf16[1024,5376]{1,0:T(8,128)(2,1)} %all-gather.2.cloned.1.call-done, bf16[5376,256]{1,0:T(8,128)(2,1)S(1)} %copy-done), kind=kOutput, calls=%fused_computation.47 | convolution fusion | flops 2818834432 | bytes 14286848 | tf_op jit(solution)/shard_map/dot_general | solution.py:67
  86.9 136.2 %while.19 = (s32[]{:T(128)}, bf16[1024,256]{1,0:T(8,128)(2,1)}, bf16[1024,256]{0,1:T(8,128)(2,1)}, f32[1536,128]{1,0:T(8,128)}, f32[1536,128]{1,0:T(8,128)}, /*i...) while((s32[]{:T(128)}, bf16[1024,256]{1,0:T(8,128)(2,1)}, ...), condition=%wide.region_4.5_spmd, body=%wide.region_0.4_spmd.sunk | while | flops 610795776 | bytes 35936128 | solution.py:126
  93.9 2.0 fusion.71
  95.9 3.1 fusion.72
  99.7 1.9 copy.90
  101.6 2.4 fusion.75
  104.0 1.9 copy.91
  107.7 1.9 copy.88
  109.6 2.2 fusion.74
  111.8 2.0 copy.89
  113.8 2.0 constant_dynamic-update-slice_fusion.9
  115.8 1.9 fusion.73
  128.0 2.0 fusion.71
  129.9 3.1 fusion.72
  133.8 1.9 copy.90
  135.7 2.4 fusion.75
  138.1 1.9 copy.91
  141.8 1.9 copy.88
  143.7 2.2 fusion.74
  145.9 2.0 copy.89
  147.8 2.0 constant_dynamic-update-slice_fusion.9
  162.0 2.0 fusion.71
  164.0 3.1 fusion.72
  167.8 1.9 copy.90
  169.7 2.4 fusion.75
  172.1 1.9 copy.91
  175.8 1.9 copy.88
  177.7 2.2 fusion.74
  179.9 2.0 copy.89
  181.9 2.0 constant_dynamic-update-slice_fusion.9
  196.1 2.0 fusion.71
  198.0 3.1 fusion.72
  201.8 1.9 copy.90
  203.8 2.4 fusion.75
  206.2 1.9 copy.91
  209.9 1.9 copy.88
  211.8 2.2 fusion.74
  214.0 2.0 copy.89
  215.9 2.1 constant_dynamic-update-slice_fusion.9
  223.2 9.7 %convolution_bitcast_fusion.2 = f32[5376,256]{0,1:T(8,128)} fusion(bf16[1024,256]{0,1:T(8,128)(2,1)} %get-tuple-element.179, bf16[1024,5376]{1,0:T(8,128)(2,1)} %all-gather.2.cloned.1.call-done), kind=kOutput, calls=%fused_computation.46 | convolution fusion | flops 2818572288 | bytes 17039360 | tf_op jit(solution)/shard_map/dot_general | solution.py:147
  232.9 6.1 %copy.66 = f32[5376,256]{1,0:T(8,128)} copy(f32[5376,256]{0,1:T(8,128)} %convolution_bitcast_fusion.2) | data formatting | bytes 11010048
  242.9 5.5 %collective-permute-done.3 = bf16[512,128]{1,0:T(8,128)(2,1)S(1)} collective-permute-done((bf16[512,128]{1,0:T(8,128)(2,1)S(1)}, bf16[512,128]{1,0:T(8,128)(2,1)S(1)}, u32[]{:S(2)}, u32[]{:S(2)}) %collective-permute-start.3) | collective-permute-done | bytes 131104 | tf_op jit(solution)/shard_map/ppermute | solution.py:15
  251.3 215.3 %reduce-scatter.4.cloned.1.call-done = f32[168,256]{1,0:T(8,128)} async-done(((f32[5376,256]{1,0:T(8,128)}), f32[168,256]{1,0:T(8,128)}) %reduce-scatter.4.cloned.1.call-update) | async-done | bytes 172048
  (130 shorter events, 71.8 us)
Async XLA Ops:
  7.2 68.2 %copy-start = (bf16[5376,256]{1,0:T(8,128)(2,1)S(1)}, bf16[5376,256]{1,0:T(8,128)(2,1)}, u32[]{:S(2)}) copy-start(bf16[5376,256]{1,0:T(8,128)(2,1)} %param.11) | copy-start | bytes 8257540
  7.2 16.3 %copy-start.7 = (bf16[1024,128]{1,0:T(8,128)(2,1)S(1)}, bf16[1024,128]{1,0:T(8,128)(2,1)}, u32[]{:S(2)}) copy-start(bf16[1024,128]{1,0:T(8,128)(2,1)} %param.8) | copy-start | bytes 786436
  7.2 17.0 %copy-start.8 = (bf16[1024,128]{1,0:T(8,128)(2,1)S(1)}, bf16[1024,128]{1,0:T(8,128)(2,1)}, u32[]{:S(2)}) copy-start(bf16[1024,128]{1,0:T(8,128)(2,1)} %param.9) | copy-start | bytes 786436
  7.2 68.2 %all-gather.2.cloned.1.call-start = ((), (), s32[]{:S(2)}) async-start(), calls=%async_computation.1 | async-start | bytes 12386304 | tf_op jit(solution)/shard_map/all_gather | solution.py:66
  7.9 458.7 %reduce-scatter.4.cloned.1.call-start = ((), (), s32[]{:S(2)}) async-start(), calls=%async_computation.2 | async-start | bytes 5677056
  8.0 11.0 %collective-permute-start = (bf16[1024,128]{1,0:T(8,128)(2,1)}, bf16[1024,128]{1,0:T(8,128)(2,1)}, u32[]{:S(2)}, u32[]{:S(2)}) collective-permute-start(bf16[1024,128]{1,0:T(8,128)(2,1)} %param.8), channel_id=1, source_target_pairs={{0,8},{8,16},{16,24},{24,32},{32,40},{40,48},{48,56},{56,64},{64,7... | collective-permute-start | bytes 786440 | tf_op jit(solution)/shard_map/ppermute | solution.py:15
  12.7 10.8 %collective-permute-start.1 = (bf16[1024,128]{1,0:T(8,128)(2,1)}, bf16[1024,128]{1,0:T(8,128)(2,1)S(1)}, u32[]{:S(2)}, u32[]{:S(2)}) collective-permute-start(bf16[1024,128]{1,0:T(8,128)(2,1)} %param.9), channel_id=1, source_target_pairs={{0,8},{8,16},{16,24},{24,32},{32,40},{40,48},{48,56},{56,64},{64,7... | collective-permute-start | bytes 786440 | tf_op jit(solution)/shard_map/ppermute | solution.py:15
  87.9 1.6 copy-start.3
  89.5 1.2 copy-start.1
  95.9 3.1 copy-start.4
  111.8 4.0 copy-start.2
  122.0 1.6 copy-start.3
  123.6 1.2 copy-start.1
  129.9 3.1 copy-start.4
  145.9 4.0 copy-start.2
  156.1 1.6 copy-start.3
  157.6 1.2 copy-start.1
  164.0 3.1 copy-start.4
  179.9 4.0 copy-start.2
  190.1 1.6 copy-start.3
  191.7 1.2 copy-start.1
  198.0 3.1 copy-start.4
  213.9 4.1 copy-start.2
  239.0 1.1 copy-start.6
  239.0 2.5 copy-start.5
  240.2 8.2 %collective-permute-start.3 = (bf16[512,128]{1,0:T(8,128)(2,1)S(1)}, bf16[512,128]{1,0:T(8,128)(2,1)S(1)}, u32[]{:S(2)}, u32[]{:S(2)}) collective-permute-start(bf16[512,128]{1,0:T(8,128)(2,1)S(1)} %get-tuple-element.249), channel_id=1, source_target_pairs={{8,0},{16,8},{24,16},{32,24},{40,32},{48,40},{56,48},{64,56},{72,6... | collective-permute-start | bytes 393224 | tf_op jit(solution)/shard_map/ppermute | solution.py:15
  241.6 9.0 %collective-permute-start.2 = (bf16[512,128]{1,0:T(8,128)(2,1)S(1)}, bf16[512,128]{1,0:T(8,128)(2,1)S(1)}, u32[]{:S(2)}, u32[]{:S(2)}) collective-permute-start(bf16[512,128]{1,0:T(8,128)(2,1)S(1)} %get-tuple-element.251), channel_id=1, source_target_pairs={{8,0},{16,8},{24,16},{32,24},{40,32},{48,40},{56,48},{64,56},{72,6... | collective-permute-start | bytes 393224 | tf_op jit(solution)/shard_map/ppermute | solution.py:15
Sparse Core Ops, SparseCore 0:
  9.9 65.4 all-gather.1
  239.1 227.4 reduce-scatter.3
where the time goes:
time: 477 us; the launch traced here: 475 us
  waiting for transfers between devices  280 us (59%)
  local copies, waits for them, and re-layouts  95.5 us (20%)
  matrix products  68.8 us (14%)
  between operations  14.2 us (3%)
  starting transfers between devices  10.5 us (2%)
  other arithmetic  5.89 us (1%)
    unnamed x3, waiting for transfers between devices  216 us
    all_gather x1, waiting for transfers between devices, shards(): grad_full = lax.all_gather(out_grad, 'mp', axis=0, tiled=True)  50.4 us
    dynamic_update_slice x8, local copies, waits for them, and re-layouts, step(): lax.dynamic_update_slice_in_dim(value_gradient_total, earlier_values + va...  16.1 us
    dynamic_slice x8, local copies, waits for them, and re-layouts, step(): lax.dynamic_slice_in_dim(value_gradient_total, start_position, WINDOW_KEY...  14.7 us
    ppermute x4, waiting for transfers between devices, shifted(): return lax.ppermute(x, axis, pairs)  13.6 us
    dynamic_slice x8, local copies, waits for them, and re-layouts, step(): lax.dynamic_slice_in_dim(output_gradient, start_position, block_index, 0)  12.9 us
    dot_general x4, matrix products, band_grads(): jnp.einsum('qhgd,khd->hgqk', output_grad_rows, value_rows_block, preferre...  12.2 us
    dynamic_slice x8, local copies, waits for them, and re-layouts, step(): lax.dynamic_slice_in_dim(key_gradient_total, start_position, WINDOW_KEYS...  10.7 us
  transfers between devices with their start and end apart: 6, of which 6 were waited for; matrix products, arithmetic and copies ran while one was open for 1% of the time, Pallas kernels for 0%

commit v1 on v0

--- a/solution.py
+++ b/solution.py
@@ -63,7 +63,9 @@
     prev_values = prev_values[shard - WINDOW_KEYS :]
     key_buf = jnp.concatenate([prev_keys, keys], 0)
     value_buf = jnp.concatenate([prev_values, values], 0)
-    grad_full = lax.all_gather(out_grad, "mp", axis=0, tiled=True)
+    grad_full = jnp.concatenate(
+        lax.all_to_all(jnp.stack([out_grad] * lax.axis_size("mp")), "mp", 0, 0), axis=0
+    )
     output_gradient = jnp.dot(grad_full, out_weight, preferred_element_type=jnp.float32).astype(
         jnp.bfloat16
     )

time: 477 us -> 543 us (1.14)
  waiting for transfers between devices: 280 us -> 334 us
  local copies, waits for them, and re-layouts: 95.5 us -> 102 us
    all_to_all x0 -> x1, waiting for transfers between devices: none -> 106 us  [shards(): lax.all_to_all(jnp.stack([out_grad] * lax.axis_size('mp')), 'mp', 0, 0)]
    all_gather x1 -> x0, waiting for transfers between devices: 50.4 us -> none  [shards(): grad_full = lax.all_gather(out_grad, 'mp', axis=0, tiled=True)]
    all_to_all x0 -> x1, starting transfers between devices: none -> 7.4 us  [shards(): lax.all_to_all(jnp.stack([out_grad] * lax.axis_size('mp')), 'mp', 0, 0)]
    another operation x2 -> x3, local copies, waits for them, and re-layouts: 1.89 us -> 8.12 us  [the longest x1 6.22 us: shards(): jnp.stack([out_grad] * lax.axis_size('mp'))]
    unnamed x3 -> x2, waiting for transfers between devices: 216 us -> 215 us
where the time goes in v1:
time: 543 us; the launch traced here: 541 us
  waiting for transfers between devices  334 us (62%)
  local copies, waits for them, and re-layouts  102 us (19%)
  matrix products  68.8 us (13%)
  starting transfers between devices  15.9 us (3%)
  between operations  14.1 us (3%)
  other arithmetic  5.94 us (1%)
    unnamed x2, waiting for transfers between devices  215 us
    all_to_all x1, waiting for transfers between devices, shards(): lax.all_to_all(jnp.stack([out_grad] * lax.axis_size('mp')), 'mp', 0, 0)  106 us
    dynamic_update_slice x8, local copies, waits for them, and re-layouts, step(): lax.dynamic_update_slice_in_dim(value_gradient_total, earlier_values + va...  16.1 us
    dynamic_slice x8, local copies, waits for them, and re-layouts, step(): lax.dynamic_slice_in_dim(value_gradient_total, start_position, WINDOW_KEY...  14.7 us
    ppermute x4, waiting for transfers between devices, shifted(): return lax.ppermute(x, axis, pairs)  13 us
    dynamic_slice x8, local copies, waits for them, and re-layouts, step(): lax.dynamic_slice_in_dim(output_gradient, start_position, block_index, 0)  12.9 us
    dot_general x4, matrix products, band_grads(): jnp.einsum('qhgd,khd->hgqk', output_grad_rows, value_rows_block, preferre...  12.2 us
  transfers between devices with their start and end apart: 6, of which 6 were waited for; matrix products, arithmetic and copies ran while one was open for 1% of the time, Pallas kernels for 0%

profile of v1, /device:TPU:8, one launch (start us, length us, event | category | flops | bytes accessed | tf_op | source)
XLA Modules:
  0.0 541.1 jit_solution(4988331626312794190)
XLA Ops:
  7.2 6.2 %stack.2 = bf16[8,128,5376]{2,1,0:T(8,128)(2,1)} broadcast(bf16[128,5376]{1,0:T(8,128)(2,1)} %param.10), dimensions={1,2} | broadcast | bytes 12386304 | tf_op jit(solution)/shard_map/stack | solution.py:67
  13.4 7.4 %all-to-all-start = ((bf16[8,128,5376]{2,1,0:T(8,128)(2,1)}), bf16[8,128,5376]{2,1,0:T(8,128)(2,1)}, u32[]{:S(2)}, u32[]{:S(2)}) async-start(bf16[8,128,5376]{2,1,0:T(8,128)(2,1)} %stack.2), calls=%async_computation | async-start | bytes 22020096 | tf_op jit(solution)/shard_map/all_to_all | solution.py:67
  20.8 2.8 collective-permute-start
  23.6 3.1 collective-permute-start.1
  26.8 2.8 collective-permute-done
  30.5 3.9 collective-permute-done.1
  36.0 106.2 %all-to-all-done = bf16[8,128,5376]{2,1,0:T(8,128)(2,1)} async-done(((bf16[8,128,5376]{2,1,0:T(8,128)(2,1)}), bf16[8,128,5376]{2,1,0:T(8,128)(2,1)}, u32[]{:S(2)}, u32[]{:S(2)}) %all-to-all-start) | async-done | bytes 11010080 | tf_op jit(solution)/shard_map/all_to_all | solution.py:67
  142.2 7.9 %convolution_convert_fusion.1 = bf16[1024,256]{1,0:T(8,128)(2,1)} fusion(bf16[1024,5376]{1,0:T(8,128)(2,1)} %bitcast.31, bf16[5376,256]{1,0:T(8,128)(2,1)S(1)} %copy-done), kind=kOutput, calls=%fused_computation.47 | convolution fusion | flops 2818834432 | bytes 14286848 | tf_op jit(solution)/shard_map/dot_general | solution.py:69
  153.7 136.3 %while.19 = (s32[]{:T(128)}, bf16[1024,256]{1,0:T(8,128)(2,1)}, bf16[1024,256]{0,1:T(8,128)(2,1)}, f32[1536,128]{1,0:T(8,128)}, f32[1536,128]{1,0:T(8,128)}, /*i...) while((s32[]{:T(128)}, bf16[1024,256]{1,0:T(8,128)(2,1)}, ...), condition=%wide.region_4.5_spmd, body=%wide.region_0.4_spmd.sunk | while | flops 610795776 | bytes 35936128 | solution.py:128
  160.7 2.0 fusion.71
  162.6 3.1 fusion.72
  166.5 1.9 copy.90
  168.4 2.4 fusion.75
  170.8 1.9 copy.91
  174.5 1.9 copy.88
  176.4 2.2 fusion.74
  178.6 2.0 copy.89
  180.6 2.0 constant_dynamic-update-slice_fusion.9
  194.7 2.0 fusion.71
  196.7 3.1 fusion.72
  200.5 1.9 copy.90
  202.4 2.4 fusion.75
  204.9 1.9 copy.91
  208.5 1.9 copy.88
  210.4 2.2 fusion.74
  212.6 2.0 copy.89
  214.6 2.1 constant_dynamic-update-slice_fusion.9
  228.8 2.0 fusion.71
  230.8 3.1 fusion.72
  234.6 1.9 copy.90
  236.5 2.4 fusion.75
  238.9 1.9 copy.91
  242.6 1.9 copy.88
  244.5 2.2 fusion.74
  246.7 2.0 copy.89
  248.7 2.0 constant_dynamic-update-slice_fusion.9
  262.9 2.0 fusion.71
  264.8 3.1 fusion.72
  268.7 1.9 copy.90
  270.6 2.4 fusion.75
  273.0 1.9 copy.91
  278.6 2.2 fusion.74
  280.8 2.0 copy.89
  282.8 2.1 constant_dynamic-update-slice_fusion.9
  290.0 9.7 %convolution_bitcast_fusion.2 = f32[5376,256]{0,1:T(8,128)} fusion(bf16[1024,256]{0,1:T(8,128)(2,1)} %get-tuple-element.179, bf16[1024,5376]{1,0:T(8,128)(2,1)} %bitcast.31), kind=kOutput, calls=%fused_computation.46 | convolution fusion | flops 2818572288 | bytes 17039360 | tf_op jit(solution)/shard_map/dot_general | solution.py:149
  299.7 6.1 %copy.66 = f32[5376,256]{1,0:T(8,128)} copy(f32[5376,256]{0,1:T(8,128)} %convolution_bitcast_fusion.2) | data formatting | bytes 11010048
  309.7 5.1 collective-permute-done.3
  317.5 215.0 %reduce-scatter.4.cloned.1.call-done = f32[168,256]{1,0:T(8,128)} async-done(((f32[5376,256]{1,0:T(8,128)}), f32[168,256]{1,0:T(8,128)}) %reduce-scatter.4.cloned.1.call-update) | async-done | bytes 172048
  (130 shorter events, 74.7 us)
Async XLA Ops:
  7.2 135.0 %copy-start = (bf16[5376,256]{1,0:T(8,128)(2,1)S(1)}, bf16[5376,256]{1,0:T(8,128)(2,1)}, u32[]{:S(2)}) copy-start(bf16[5376,256]{1,0:T(8,128)(2,1)} %param.11) | copy-start | bytes 8257540
  13.4 7.4 %copy-start.7 = (bf16[1024,128]{1,0:T(8,128)(2,1)S(1)}, bf16[1024,128]{1,0:T(8,128)(2,1)}, u32[]{:S(2)}) copy-start(bf16[1024,128]{1,0:T(8,128)(2,1)} %param.8) | copy-start | bytes 786436
  13.4 10.2 %copy-start.8 = (bf16[1024,128]{1,0:T(8,128)(2,1)S(1)}, bf16[1024,128]{1,0:T(8,128)(2,1)}, u32[]{:S(2)}) copy-start(bf16[1024,128]{1,0:T(8,128)(2,1)} %param.9) | copy-start | bytes 786436
  13.4 128.8 %all-to-all-start = ((bf16[8,128,5376]{2,1,0:T(8,128)(2,1)}), bf16[8,128,5376]{2,1,0:T(8,128)(2,1)}, u32[]{:S(2)}, u32[]{:S(2)}) async-start(bf16[8,128,5376]{2,1,0:T(8,128)(2,1)} %stack.2), calls=%async_computation | async-start | bytes 22020096 | tf_op jit(solution)/shard_map/all_to_all | solution.py:67
  20.8 511.7 %reduce-scatter.4.cloned.1.call-start = ((), (), s32[]{:S(2)}) async-start(), calls=%async_computation.2 | async-start | bytes 5677056
  20.8 8.7 %collective-permute-start = (bf16[1024,128]{1,0:T(8,128)(2,1)S(1)}, bf16[1024,128]{1,0:T(8,128)(2,1)}, u32[]{:S(2)}, u32[]{:S(2)}) collective-permute-start(bf16[1024,128]{1,0:T(8,128)(2,1)S(1)} %copy-done.7), channel_id=1, source_target_pairs={{0,8},{8,16},{16,24},{24,32},{32,40},{40,48},{48,56},{56,64},{64,7... | collective-permute-start | bytes 786440 | tf_op jit(solution)/shard_map/ppermute | solution.py:15
  23.6 10.8 %collective-permute-start.1 = (bf16[1024,128]{1,0:T(8,128)(2,1)S(1)}, bf16[1024,128]{1,0:T(8,128)(2,1)S(1)}, u32[]{:S(2)}, u32[]{:S(2)}) collective-permute-start(bf16[1024,128]{1,0:T(8,128)(2,1)S(1)} %copy-done.8), channel_id=1, source_target_pairs={{0,8},{8,16},{16,24},{24,32},{32,40},{40,48},{48,56},{56,64},{64,7... | collective-permute-start | bytes 786440 | tf_op jit(solution)/shard_map/ppermute | solution.py:15
  154.7 1.6 copy-start.3
  156.3 1.2 copy-start.1
  162.6 3.1 copy-start.4
  178.6 4.0 copy-start.2
  188.8 1.6 copy-start.3
  190.3 1.2 copy-start.1
  196.7 3.1 copy-start.4
  212.6 4.0 copy-start.2
  222.9 1.6 copy-start.3
  224.4 1.2 copy-start.1
  230.8 3.1 copy-start.4
  246.7 4.0 copy-start.2
  256.9 1.6 copy-start.3
  258.5 1.2 copy-start.1
  264.8 3.1 copy-start.4
  280.8 4.1 copy-start.2
  305.8 1.1 copy-start.6
  305.8 2.5 copy-start.5
  307.0 7.8 %collective-permute-start.3 = (bf16[512,128]{1,0:T(8,128)(2,1)S(1)}, bf16[512,128]{1,0:T(8,128)(2,1)S(1)}, u32[]{:S(2)}, u32[]{:S(2)}) collective-permute-start(bf16[512,128]{1,0:T(8,128)(2,1)S(1)} %get-tuple-element.249), channel_id=1, source_target_pairs={{8,0},{16,8},{24,16},{32,24},{40,32},{48,40},{56,48},{64,56},{72,6... | collective-permute-start | bytes 393224 | tf_op jit(solution)/shard_map/ppermute | solution.py:15
  308.4 8.4 %collective-permute-start.2 = (bf16[512,128]{1,0:T(8,128)(2,1)S(1)}, bf16[512,128]{1,0:T(8,128)(2,1)S(1)}, u32[]{:S(2)}, u32[]{:S(2)}) collective-permute-start(bf16[512,128]{1,0:T(8,128)(2,1)S(1)} %get-tuple-element.251), channel_id=1, source_target_pairs={{8,0},{16,8},{24,16},{32,24},{40,32},{48,40},{56,48},{64,56},{72,6... | collective-permute-start | bytes 393224 | tf_op jit(solution)/shard_map/ppermute | solution.py:15
Sparse Core Ops, SparseCore 0:
  306.0 226.5 reduce-scatter.3
